TPU v7x, 32 devices: a whole 2x2x4 slice. The times are simulated.
32 devices in a mesh: row: 4 (over x, core), col: 8 (over z, y).
Axes of the slice: x: 2, y: 2, z: 4, core: 2. Of those that a mesh axis runs over, the one named last changes fastest.
Arguments:
- amplitudes: bfloat16 [640, 90000], P(('row', 'col')), may hold values from -6 to 6
- coulomb: bfloat16 [90000, 8192], P('col', 'row'), may hold values from -0.01953125 to 0.01953125
Outputs:
- ladder: float32 [640, 8192], P('col', 'row')
All inputs are finite; a program needn't handle non-finite values.
Results may differ from a plain program's by a relative error of at most 0.0003.
Values may be sent and summed in bfloat16 or wider, within the bound.
A program may use at most 192 MiB of HBM per device.

v0:
```python
import jax
import jax.numpy as jnp
from jax import lax
from jax.sharding import PartitionSpec as P


def shards(amplitudes, coulomb):
    columns = lax.axis_size("col")
    grid_rows = lax.axis_size("row")
    pairs_here = amplitudes.shape[0]
    gathered = lax.all_gather(amplitudes, "row", axis=0, tiled=True)
    divided = lax.all_to_all(gathered, "col", split_axis=1, concat_axis=0, tiled=True)
    amp_panel = (
        divided.reshape(columns, grid_rows, pairs_here, -1)
        .transpose(1, 0, 2, 3)
        .reshape(columns * grid_rows * pairs_here, -1)
    )
    contraction = lax.psum_scatter(
        jnp.dot(amp_panel, coulomb, preferred_element_type=jnp.float32),
        "col",
        scatter_dimension=0,
        tiled=True,
    )
    return 0.5 * contraction


def solution(mesh):
    return jax.shard_map(
        shards,
        mesh=mesh,
        in_specs=(P(("row", "col"), None), P("col", "row")),
        out_specs=P("col", "row"),
        check_vma=False,
    )
```

profile of v0, /device:TPU:0, one launch (start us, length us, event | category | flops | bytes accessed | tf_op | source)
XLA Modules:
  0.0 709.9 jit_solution(15192235803599281325)
XLA Ops:
  6.5 0.0 all-gather.3.cloned.1.call-start
  6.5 0.7 all-gather.3.cloned.1.call-update
  7.3 0.0 reduce-scatter.2.cloned.1.call-start
  7.3 115.6 %all-gather.3.cloned.1.call-done = bf16[4,20,90000]{2,1,0:T(8,128)(2,1)} async-done(((bf16[1,20,90000]{2,1,0:T(8,128)(2,1)}), bf16[4,20,90000]{2,1,0:T(8,128)(2,1)}) %all-gather.3.cloned.1.call-update) | async-done | bytes 14400016 | tf_op jit(solution)/shard_map/all_gather | solution.py:11
  122.9 39.6 %all_to_all.12 = bf16[80,8,11250]{2,1,0:T(8,128)(2,1)} reshape(bf16[4,20,90000]{2,1,0:T(8,128)(2,1)} %all-gather.3.cloned.1.call-done) | data formatting | bytes 28800000 | tf_op jit(solution)/shard_map/all_to_all | solution.py:12
  162.6 9.2 %copy.6 = bf16[80,8,11250]{2,0,1:T(8,128)(2,1)S(1)} copy(bf16[80,8,11250]{2,1,0:T(8,128)(2,1)} %all_to_all.12) | data formatting | bytes 28800000 | tf_op jit(solution)/shard_map/all_to_all | solution.py:12
  171.8 318.0 %all_to_all.16 = bf16[80,8,11250]{2,0,1:T(8,128)(2,1)S(1)} all-to-all(bf16[80,8,11250]{2,0,1:T(8,128)(2,1)S(1)} %copy.6), channel_id=1, replica_groups=mesh['row'=4,'col'=8] {'col'}, dimensions={1} | all-to-all | bytes 28800000 | tf_op jit(solution)/shard_map/all_to_all | solution.py:12
  489.8 29.1 %copy.7 = bf16[80,8,11250]{2,1,0:T(8,128)(2,1)S(1)} copy(bf16[80,8,11250]{2,0,1:T(8,128)(2,1)S(1)} %all_to_all.16) | data formatting | bytes 28800000 | tf_op jit(solution)/shard_map/all_to_all | solution.py:12
  518.8 23.8 %copy.8 = bf16[4,8,20,11250]{3,2,1,0:T(8,128)(2,1)} copy(bf16[4,8,20,11250]{3,1,2,0:T(8,128)(2,1)S(1)} %bitcast.8) | data formatting | bytes 28800000 | tf_op jit(solution)/shard_map/transpose | solution.py:15
  542.7 19.0 %reshape.11 = bf16[640,11250]{1,0:T(8,128)(2,1)} reshape(bf16[4,8,20,11250]{3,2,1,0:T(8,128)(2,1)} %copy.8) | data formatting | bytes 28800000 | tf_op jit(solution)/shard_map/reshape | solution.py:16
  561.7 38.1 %fusion = f32[640,2048]{1,0:T(8,128)} fusion(bf16[640,11250]{1,0:T(8,128)(2,1)} %reshape.11, bf16[11250,2048]{1,0:T(8,128)(2,1)} %param.3), kind=kOutput, calls=%fused_computation.1 | convolution fusion | flops 29491200000 | bytes 65722880 | tf_op jit(solution)/shard_map/dot_general | solution.py:19
  599.8 0.0 reduce-scatter.2.cloned.1.call-update
  599.8 101.3 %reduce-scatter.2.cloned.1.call-done = f32[80,2048]{1,0:T(8,128)} async-done(((f32[640,2048]{1,0:T(8,128)}), f32[80,2048]{1,0:T(8,128)}) %reduce-scatter.2.cloned.1.call-update) | async-done | bytes 655376 | tf_op jit(solution)/shard_map/reduce_scatter | solution.py:18
  701.1 2.0 broadcast_multiply_fusion
Async XLA Ops:
  6.5 116.4 %all-gather.3.cloned.1.call-start = ((), (), s32[]{:S(2)}) async-start(), calls=%async_computation.3 | async-start | bytes 21626880 | tf_op jit(solution)/shard_map/all_gather | solution.py:11
  7.3 693.8 %reduce-scatter.2.cloned.1.call-start = ((), (), s32[]{:S(2)}) async-start(), calls=%async_computation.2 | async-start | bytes 5898240 | tf_op jit(solution)/shard_map/reduce_scatter | solution.py:18
Sparse Core Ops, SparseCore 0:
  8.9 113.9 all-gather.2
  599.9 101.1 reduce-scatter.1
where the time goes:
time: 711 us; the launch traced here: 710 us
  blocking collectives  318 us (45%)
  waiting for transfers between devices  218 us (31%)
  local copies, waits for them, and re-layouts  121 us (17%)
  matrix products  38.1 us (5%)
  between operations  13.4 us (2%)
    all_to_all x1, blocking collectives, shards(): lax.all_to_all(gathered, 'col', split_axis=1, concat_axis=0, tiled=True)  318 us
    all_gather x1, waiting for transfers between devices, shards(): gathered = lax.all_gather(amplitudes, 'row', axis=0, tiled=True)  116 us
    reduce_scatter x1, waiting for transfers between devices, shards(): lax.psum_scatter(jnp.dot(amp_panel, coulomb, preferred_element_type=jnp.f...  101 us
    all_to_all x3, local copies, waits for them, and re-layouts, shards(): lax.all_to_all(gathered, 'col', split_axis=1, concat_axis=0, tiled=True)  77.9 us
    dot_general x1, matrix products, shards(): jnp.dot(amp_panel, coulomb, preferred_element_type=jnp.float32)  38.1 us
    transpose x1, local copies, waits for them, and re-layouts, shards(): amp_panel = divided.reshape(columns, grid_rows, pairs_here, -1).transpose...  23.8 us
    reshape x1, local copies, waits for them, and re-layouts, shards(): amp_panel = divided.reshape(columns, grid_rows, pairs_here, -1).transpose...  19 us
  transfers between devices with their start and end apart: 2, of which 2 were waited for; matrix products, arithmetic and copies ran while one was open for 0% of the time, Pallas kernels for 0%

commit v1 on v0

--- a/solution.py
+++ b/solution.py
@@ -4,11 +4,28 @@
 from jax.sharding import PartitionSpec as P
 
 
+def laid_out(blocks, dim):
+    blocks = jnp.moveaxis(blocks, 0, dim)
+    shape = blocks.shape
+    return blocks.reshape(*shape[:dim], shape[dim] * shape[dim + 1], *shape[dim + 2 :])
+
+
+def doubled(array, axis):
+    peers, index = (lax.axis_size(axis), lax.axis_index(axis))
+    blocks, stride = (array[None], 1)
+    while stride < peers:
+        other = lax.ppermute(blocks, axis, [(i, i ^ stride) for i in range(peers)])
+        low = index & stride == 0
+        blocks = jnp.concatenate([jnp.where(low, blocks, other), jnp.where(low, other, blocks)])
+        stride *= 2
+    return blocks
+
+
 def shards(amplitudes, coulomb):
     columns = lax.axis_size("col")
     grid_rows = lax.axis_size("row")
     pairs_here = amplitudes.shape[0]
-    gathered = lax.all_gather(amplitudes, "row", axis=0, tiled=True)
+    gathered = laid_out(doubled(amplitudes, "row"), 0)
     divided = lax.all_to_all(gathered, "col", split_axis=1, concat_axis=0, tiled=True)
     amp_panel = (
         divided.reshape(columns, grid_rows, pairs_here, -1)

time: 711 us -> 809 us (1.14)
  waiting for transfers between devices: 218 us -> 265 us
  other arithmetic: 1.97 us -> 38.1 us
  local copies, waits for them, and re-layouts: 121 us -> 133 us
    ppermute x0 -> x2, waiting for transfers between devices: none -> 163 us  [doubled(): other = lax.ppermute(blocks, axis, [(i, i ^ stride) for i in range(peers)])]
    all_gather x1 -> x0, waiting for transfers between devices: 116 us -> none  [shards(): gathered = lax.all_gather(amplitudes, 'row', axis=0, tiled=True)]
    select_n x0 -> x2, other arithmetic: none -> 18.6 us  [doubled(): jnp.where(low, blocks, other)]
    concatenate x0 -> x2, other arithmetic: none -> 17.5 us  [doubled(): jnp.concatenate([jnp.where(low, blocks, other), jnp.where(low, other, blo...]
    concatenate x0 -> x1, local copies, waits for them, and re-layouts: none -> 11.8 us  [doubled(): jnp.concatenate([jnp.where(low, blocks, other), jnp.where(low, other, blo...]
  transfers between devices with their start and end apart: 2 -> 3, of which waited for: 2 -> 3; matrix products, arithmetic and copies ran while one was open for 0% -> 0% of each run, Pallas kernels for 0% -> 0%
where the time goes in v1:
time: 809 us; the launch traced here: 808 us
  blocking collectives  318 us (39%)
  waiting for transfers between devices  265 us (33%)
  local copies, waits for them, and re-layouts  133 us (16%)
  other arithmetic  38.1 us (5%)
  matrix products  38.1 us (5%)
  between operations  13.4 us (2%)
    all_to_all x1, blocking collectives, shards(): lax.all_to_all(gathered, 'col', split_axis=1, concat_axis=0, tiled=True)  318 us
    ppermute x2, waiting for transfers between devices, doubled(): other = lax.ppermute(blocks, axis, [(i, i ^ stride) for i in range(peers)])  163 us
    reduce_scatter x1, waiting for transfers between devices, shards(): lax.psum_scatter(jnp.dot(amp_panel, coulomb, preferred_element_type=jnp.f...  101 us
    all_to_all x3, local copies, waits for them, and re-layouts, shards(): lax.all_to_all(gathered, 'col', split_axis=1, concat_axis=0, tiled=True)  77.9 us
    dot_general x1, matrix products, shards(): jnp.dot(amp_panel, coulomb, preferred_element_type=jnp.float32)  38.1 us
    transpose x1, local copies, waits for them, and re-layouts, shards(): amp_panel = divided.reshape(columns, grid_rows, pairs_here, -1).transpose...  23.8 us
    reshape x1, local copies, waits for them, and re-layouts, shards(): amp_panel = divided.reshape(columns, grid_rows, pairs_here, -1).transpose...  19 us
    select_n x2, other arithmetic, doubled(): jnp.where(low, blocks, other)  18.6 us
  transfers between devices with their start and end apart: 3, of which 3 were waited for; matrix products, arithmetic and copies ran while one was open for 0% of the time, Pallas kernels for 0%

profile of v1, /device:TPU:0, one launch (start us, length us, event | category | flops | bytes accessed | tf_op | source)
XLA Modules:
  0.0 808.3 jit_solution(11204823487345116395)
XLA Ops:
  6.5 0.0 reduce-scatter.2.cloned.1.call-start
  6.5 0.5 collective-permute-start
  7.0 7.3 collective-permute-done
  14.3 6.1 broadcast_select_fusion.3
  20.4 0.0 copy-start
  20.5 8.3 %pad_maximum_fusion.1 = bf16[2,20,90000]{2,1,0:T(8,128)(2,1)} fusion(bf16[1,20,90000]{2,1,0:T(8,128)(2,1)} %get-tuple-element.8, bf16[1,20,90000]{2,1,0:T(8,128)(2,1)S(1)} %get-tuple-element.7), kind=kLoop, calls=%fused_computation.1 | loop fusion | flops 3600000 | bytes 14400000 | tf_op jit(solution)/shard_map/concatenate | solution.py:19
  28.7 0.0 copy-done
  28.7 11.8 %copy.7 = bf16[2,20,90000]{2,0,1:T(2,128)(2,1)} copy(bf16[2,20,90000]{2,1,0:T(8,128)(2,1)} %pad_maximum_fusion.1) | data formatting | bytes 14400000 | tf_op jit(solution)/shard_map/concatenate | solution.py:19
  40.5 2.8 collective-permute-start.1
  43.4 155.8 %collective-permute-done.1 = bf16[2,20,90000]{2,0,1:T(2,128)(2,1)} collective-permute-done((bf16[2,20,90000]{2,0,1:T(2,128)(2,1)}, bf16[2,20,90000]{2,0,1:T(2,128)(2,1)}, u32[]{:S(2)}, u32[]{:S(2)}) %collective-permute-start.1) | collective-permute-done | bytes 7200032 | tf_op jit(solution)/shard_map/ppermute | solution.py:17
  199.2 12.5 %broadcast_select_fusion.1 = (bf16[2,20,90000]{2,1,0:T(8,128)(2,1)S(1)}, bf16[2,20,90000]{2,1,0:T(8,128)(2,1)S(1)}) fusion(pred[]{:T(512)S(6)} %eq.6, bf16[2,20,90000]{2,0,1:T(2,128)(2,1)} %collective-permute-done.1, bf16[1,20,90000]{2,1,0:T(8,128)(2,1)} %get-tuple-element.8, bf16[1,20,90000]{2,1,0:T(8,128)(2,1)} %copy-done), kind=kLoop, calls=%fused_computation.3 | loop fusion | flops 10800000 | bytes 28800000 | tf_op jit(solution)/shard_map/jit(_where)/select_n | solution.py:19
  211.6 9.2 %pad_maximum_fusion = bf16[4,20,90000]{2,1,0:T(8,128)(2,1)} fusion(bf16[2,20,90000]{2,1,0:T(8,128)(2,1)S(1)} %get-tuple-element.6, bf16[2,20,90000]{2,1,0:T(8,128)(2,1)S(1)} %get-tuple-element.5), kind=kLoop, calls=%fused_computation | loop fusion | flops 7200000 | bytes 28800000 | tf_op jit(solution)/shard_map/concatenate | solution.py:19
  220.9 39.7 %all_to_all.12 = bf16[80,8,11250]{2,1,0:T(8,128)(2,1)} reshape(bf16[4,20,90000]{2,1,0:T(8,128)(2,1)} %pad_maximum_fusion) | data formatting | bytes 28800000 | tf_op jit(solution)/shard_map/all_to_all | solution.py:29
  260.5 9.2 %copy.10 = bf16[80,8,11250]{2,0,1:T(8,128)(2,1)S(1)} copy(bf16[80,8,11250]{2,1,0:T(8,128)(2,1)} %all_to_all.12) | data formatting | bytes 28800000 | tf_op jit(solution)/shard_map/all_to_all | solution.py:29
  269.7 318.3 %all_to_all.16 = bf16[80,8,11250]{2,0,1:T(8,128)(2,1)S(1)} all-to-all(bf16[80,8,11250]{2,0,1:T(8,128)(2,1)S(1)} %copy.10), channel_id=1, replica_groups=mesh['row'=4,'col'=8] {'col'}, dimensions={1} | all-to-all | bytes 28800000 | tf_op jit(solution)/shard_map/all_to_all | solution.py:29
  588.0 29.1 %copy.11 = bf16[80,8,11250]{2,1,0:T(8,128)(2,1)S(1)} copy(bf16[80,8,11250]{2,0,1:T(8,128)(2,1)S(1)} %all_to_all.16) | data formatting | bytes 28800000 | tf_op jit(solution)/shard_map/all_to_all | solution.py:29
  617.1 23.8 %copy.12 = bf16[4,8,20,11250]{3,2,1,0:T(8,128)(2,1)} copy(bf16[4,8,20,11250]{3,1,2,0:T(8,128)(2,1)S(1)} %bitcast.10) | data formatting | bytes 28800000 | tf_op jit(solution)/shard_map/transpose | solution.py:32
  640.9 19.0 %reshape.13 = bf16[640,11250]{1,0:T(8,128)(2,1)} reshape(bf16[4,8,20,11250]{3,2,1,0:T(8,128)(2,1)} %copy.12) | data formatting | bytes 28800000 | tf_op jit(solution)/shard_map/reshape | solution.py:33
  659.9 38.1 %fusion = f32[640,2048]{1,0:T(8,128)} fusion(bf16[640,11250]{1,0:T(8,128)(2,1)} %reshape.13, bf16[11250,2048]{1,0:T(8,128)(2,1)} %param.3), kind=kOutput, calls=%fused_computation.7 | convolution fusion | flops 29491200000 | bytes 65722880 | tf_op jit(solution)/shard_map/dot_general | solution.py:36
  698.0 0.0 reduce-scatter.2.cloned.1.call-update
  698.1 101.4 %reduce-scatter.2.cloned.1.call-done = f32[80,2048]{1,0:T(8,128)} async-done(((f32[640,2048]{1,0:T(8,128)}), f32[80,2048]{1,0:T(8,128)}) %reduce-scatter.2.cloned.1.call-update) | async-done | bytes 655376 | tf_op jit(solution)/shard_map/reduce_scatter | solution.py:35
  799.5 2.0 broadcast_multiply_fusion
Async XLA Ops:
  6.5 793.0 %reduce-scatter.2.cloned.1.call-start = ((), (), s32[]{:S(2)}) async-start(), calls=%async_computation.2 | async-start | bytes 5898240 | tf_op jit(solution)/shard_map/reduce_scatter | solution.py:35
  6.5 7.8 collective-permute-start
  20.4 8.3 %copy-start = (bf16[1,20,90000]{2,1,0:T(8,128)(2,1)}, bf16[1,20,90000]{2,1,0:T(8,128)(2,1)S(1)}, u32[]{:S(2)}) copy-start(bf16[1,20,90000]{2,1,0:T(8,128)(2,1)S(1)} %get-tuple-element.7) | copy-start | bytes 10800004
  40.5 158.6 %collective-permute-start.1 = (bf16[2,20,90000]{2,0,1:T(2,128)(2,1)}, bf16[2,20,90000]{2,0,1:T(2,128)(2,1)}, u32[]{:S(2)}, u32[]{:S(2)}) collective-permute-start(bf16[2,20,90000]{2,0,1:T(2,128)(2,1)} %copy.7), channel_id=1, source_target_pairs={{0,16},{8,24},{16,0},{24,8},{1,17},{9,25},{17,1},{25,9},{2,18},{10... | collective-permute-start | bytes 21600008 | tf_op jit(solution)/shard_map/ppermute | solution.py:17
Sparse Core Ops, SparseCore 0:
  698.2 101.2 reduce-scatter.1
